TPU v7x, 32 devices: a whole 2x2x4 slice. The times are simulated.
32 devices in a mesh: rows: 2 (over x), feat: 16 (over z, y, core).
Axes of the slice: x: 2, y: 2, z: 4, core: 2. Of those that a mesh axis runs over, the one named last changes fastest.
Arguments:
- slab_grads: bfloat16 [448, 262144], P('rows', 'feat'), may hold values from -6 to 6
- basis: bfloat16 [262144, 1024], P('feat', 'rows'), may hold values from -0.01171875 to 0.01171875
- eigenvalues: float32 [1024], replicated, may hold values from 0.02 to 2
- store_rows: bfloat16 [16384, 1024], P(('rows', 'feat')), may hold values from -0.1875 to 0.1875
- slab_index: int32 [448], replicated, may hold values from 0 to 16383
Outputs:
- scores: float32 [448, 16384], P(None, ('rows', 'feat'))
All inputs are finite; a program needn't handle non-finite values.
Results may differ from a plain program's by a relative error of at most 0.0029.
Values may be sent and summed in bfloat16 or wider, within the bound.
No kernel may reach another device: no remote copies, remote signals or barrier semaphores. Data moves between devices by JAX's collectives and lax.ppermute only.
A program may use at most 128 MiB of HBM per device.

v0:
```python
import jax
import jax.numpy as jnp
from jax import lax
from jax.sharding import PartitionSpec as P

DAMPING = 0.1


def shards(slab_grads, basis, eigenvalues, store_rows, slab_index):
    feat_groups = lax.axis_size("feat")
    store_count = store_rows.shape[0]
    first_column = (lax.axis_index("rows") * feat_groups + lax.axis_index("feat")) * store_count
    columns = first_column + jnp.arange(store_count, dtype=jnp.int32)
    local_dirs = basis.shape[1]
    partial_value = jnp.dot(
        lax.all_gather(slab_grads, "rows", axis=0, tiled=True),
        basis,
        preferred_element_type=jnp.float32,
    )
    summed = lax.psum(partial_value, "feat")
    scales = lax.dynamic_slice_in_dim(
        eigenvalues, lax.axis_index("rows") * local_dirs, local_dirs, 0
    )
    whitened = (summed / (scales + DAMPING)).astype(jnp.bfloat16)
    gathered = lax.all_gather(whitened, "rows", axis=1, tiled=True)
    product = lax.dot_general(
        gathered, store_rows, (((1,), (1,)), ((), ())), preferred_element_type=jnp.float32
    )
    return jnp.where(slab_index[:, None] == columns[None, :], jnp.zeros_like(product), product)


def solution(mesh):
    in_specs = (P("rows", "feat"), P("feat", "rows"), P(), P(("rows", "feat"), None), P())
    out_specs = P(None, ("rows", "feat"))
    return jax.shard_map(shards, mesh=mesh, in_specs=in_specs, out_specs=out_specs, check_vma=False)
```

profile of v0, /device:TPU:0, one launch (start us, length us, event | category | flops | bytes accessed | tf_op | source)
XLA Modules:
  0.0 319.1 jit_solution(506024882513834059)
XLA Ops:
  6.5 0.0 copy-start
  6.5 0.0 all-gather.2.cloned.1.call-start
  6.5 0.7 all-gather.2.cloned.1.call-update
  7.3 0.0 copy-start.1
  7.3 0.0 copy-start.2
  7.3 0.0 all-reduce.2.cloned.1.call-start
  7.3 179.8 %all-gather.2.cloned.1.call-done = bf16[448,16384]{1,0:T(8,128)(2,1)} async-done(((bf16[224,16384]{1,0:T(8,128)(2,1)}), bf16[448,16384]{1,0:T(8,128)(2,1)}) %all-gather.2.cloned.1.call-update) | async-done | bytes 14680080 | tf_op jit(solution)/shard_map/all_gather | solution.py:16
  187.2 16.5 %fusion = f32[448,512]{1,0:T(8,128)} fusion(bf16[448,16384]{1,0:T(8,128)(2,1)} %all-gather.2.cloned.1.call-done, bf16[16384,512]{1,0:T(8,128)(2,1)} %param.6), kind=kOutput, calls=%fused_computation.4 | convolution fusion | flops 7516192768 | bytes 32374784 | tf_op jit(solution)/shard_map/dot_general | solution.py:15
  203.7 0.0 all-reduce.2.cloned.1.call-update
  203.7 0.0 copy-done.1
  203.7 0.1 dynamic-slice_add_fusion
  203.8 92.3 %all-reduce.2.cloned.1.call-done = f32[448,512]{1,0:T(8,128)} async-done(((f32[448,512]{1,0:T(8,128)}), f32[448,512]{1,0:T(8,128)}) %all-reduce.2.cloned.1.call-update) | async-done | bytes 917520 | tf_op jit(solution)/shard_map/psum | solution.py:20
  296.1 1.3 divide_convert_fusion
  297.4 13.2 %all_gather.7 = bf16[448,1024]{1,0:T(8,128)(2,1)S(1)} all-gather(bf16[448,512]{1,0:T(8,128)(2,1)S(1)} %divide_convert_fusion), channel_id=1, replica_groups=mesh['rows'=2,'feat'=16] {'rows'}, dimensions={1}, use_global_device_ids=true | all-gather | bytes 1376256 | tf_op jit(solution)/shard_map/all_gather | solution.py:25
  310.7 0.0 copy-done
  310.7 0.0 copy-done.2
  310.7 1.6 convolution_select_fusion
  (1 shorter events, 0.0 us)
Async XLA Ops:
  6.5 304.1 %copy-start = (bf16[512,1024]{1,0:T(8,128)(2,1)S(1)}, bf16[512,1024]{1,0:T(8,128)(2,1)}, u32[]{:S(2)}) copy-start(bf16[512,1024]{1,0:T(8,128)(2,1)} %param.8) | copy-start | bytes 3145732
  6.5 180.6 %all-gather.2.cloned.1.call-start = ((), (), s32[]{:S(2)}) async-start(), calls=%async_computation | async-start | bytes 22020096 | tf_op jit(solution)/shard_map/all_gather | solution.py:16
  7.3 196.5 %copy-start.1 = (f32[1024]{0:T(1024)S(1)}, f32[1024]{0:T(1024)}, u32[]{:S(2)}) copy-start(f32[1024]{0:T(1024)} %param.7) | copy-start | bytes 12292
  7.3 303.4 %copy-start.2 = (s32[448]{0:T(512)S(1)}, s32[448]{0:T(512)}, u32[]{:S(2)}) copy-start(s32[448]{0:T(512)} %param.9) | copy-start | bytes 5380
  7.3 288.9 %all-reduce.2.cloned.1.call-start = ((), (), s32[]{:S(2)}) async-start(), calls=%async_computation.1 | async-start | bytes 1835008 | tf_op jit(solution)/shard_map/psum | solution.py:20
Sparse Core Ops, SparseCore 0:
  8.9 178.2 all-gather.1
  203.8 92.2 all-reduce.1
where the time goes:
time: 319 us
  waiting for transfers between devices  273 us (86%)
  matrix products  18.1 us (6%)
  between operations  13.4 us (4%)
  blocking collectives  13.2 us (4%)
    all_gather x1, waiting for transfers between devices, shards(): lax.all_gather(slab_grads, 'rows', axis=0, tiled=True)  180 us
    psum x1, waiting for transfers between devices, shards(): summed = lax.psum(partial_value, 'feat')  92.3 us
    dot_general x1, matrix products, shards(): jnp.dot(lax.all_gather(slab_grads, 'rows', axis=0, tiled=True), basis, pr...  16.5 us
    all_gather x1, blocking collectives, shards(): gathered = lax.all_gather(whitened, 'rows', axis=1, tiled=True)  13.2 us
  transfers between devices with their start and end apart: 2, of which 2 were waited for; matrix products, arithmetic and copies ran while one was open for 0% of the time, Pallas kernels for 0%

commit v1 on v0

--- a/solution.py
+++ b/solution.py
@@ -4,6 +4,10 @@
 from jax.sharding import PartitionSpec as P
 
 DAMPING = 0.1
+
+
+def form_the_records(matrix):
+    return jnp.sum(jax.lax.all_gather(matrix, axis_name="feat"), axis=0)
 
 
 def shards(slab_grads, basis, eigenvalues, store_rows, slab_index):
@@ -17,7 +21,7 @@
         basis,
         preferred_element_type=jnp.float32,
     )
-    summed = lax.psum(partial_value, "feat")
+    summed = form_the_records(partial_value)
     scales = lax.dynamic_slice_in_dim(
         eigenvalues, lax.axis_index("rows") * local_dirs, local_dirs, 0
     )

time: 319 us -> 346 us (1.085)
  waiting for transfers between devices: 273 us -> 294 us
  other arithmetic: 1.36 us -> 7.26 us
    all_gather x0 -> x1, waiting for transfers between devices: none -> 113 us  [form_the_records(): return jnp.sum(jax.lax.all_gather(matrix, axis_name='feat'), axis=0)]
    psum x1 -> x0, waiting for transfers between devices: 92.3 us -> none  [shards(): summed = lax.psum(partial_value, 'feat')]
    reduce_sum x0 -> x1, other arithmetic: none -> 7.07 us  [form_the_records(): return jnp.sum(jax.lax.all_gather(matrix, axis_name='feat'), axis=0)]
where the time goes in v1:
time: 346 us
  waiting for transfers between devices  294 us (85%)
  matrix products  18.1 us (5%)
  between operations  13.4 us (4%)
  blocking collectives  13.3 us (4%)
  other arithmetic  7.26 us (2%)
    all_gather x1, waiting for transfers between devices, shards(): lax.all_gather(slab_grads, 'rows', axis=0, tiled=True)  180 us
    all_gather x1, waiting for transfers between devices, form_the_records(): return jnp.sum(jax.lax.all_gather(matrix, axis_name='feat'), axis=0)  113 us
    dot_general x1, matrix products, shards(): jnp.dot(lax.all_gather(slab_grads, 'rows', axis=0, tiled=True), basis, pr...  16.5 us
    all_gather x1, blocking collectives, shards(): gathered = lax.all_gather(whitened, 'rows', axis=1, tiled=True)  13.3 us
    reduce_sum x1, other arithmetic, form_the_records(): return jnp.sum(jax.lax.all_gather(matrix, axis_name='feat'), axis=0)  7.07 us
  transfers between devices with their start and end apart: 2, of which 2 were waited for; matrix products, arithmetic and copies ran while one was open for 0% of the time, Pallas kernels for 0%

profile of v1, /device:TPU:0, one launch (start us, length us, event | category | flops | bytes accessed | tf_op | source)
XLA Modules:
  0.0 346.2 jit_solution(12851687484744743087)
XLA Ops:
  6.5 0.0 copy-start
  6.5 0.0 all-gather.4.cloned.1.call-start
  6.5 0.7 all-gather.4.cloned.1.call-update
  7.3 0.0 copy-start.1
  7.3 0.0 all-gather.6.cloned.1.call-start
  7.3 179.8 %all-gather.4.cloned.1.call-done = bf16[448,16384]{1,0:T(8,128)(2,1)} async-done(((bf16[224,16384]{1,0:T(8,128)(2,1)}), bf16[448,16384]{1,0:T(8,128)(2,1)}) %all-gather.4.cloned.1.call-update) | async-done | bytes 14680080 | tf_op jit(solution)/shard_map/all_gather | solution.py:20
  187.2 16.5 %fusion = f32[448,512]{1,0:T(8,128)} fusion(bf16[448,16384]{1,0:T(8,128)(2,1)} %all-gather.4.cloned.1.call-done, bf16[16384,512]{1,0:T(8,128)(2,1)} %param.6), kind=kOutput, calls=%fused_computation.4 | convolution fusion | flops 7516192768 | bytes 32374784 | tf_op jit(solution)/shard_map/dot_general | solution.py:19
  203.7 0.0 copy-start.2
  203.7 0.0 all-gather.6.cloned.1.call-update
  203.7 0.0 copy-done.1
  203.7 0.1 dynamic-slice_add_fusion
  203.8 113.4 %all-gather.6.cloned.1.call-done = f32[7168,512]{1,0:T(8,128)} async-done(((f32[448,512]{1,0:T(8,128)}), f32[7168,512]{1,0:T(8,128)}) %all-gather.6.cloned.1.call-update) | async-done | bytes 14680080 | tf_op jit(solution)/shard_map/all_gather | solution.py:10
  317.2 7.1 %reduce_sum.9 = f32[448,512]{1,0:T(8,128)S(1)} reduce(f32[16,448,512]{2,1,0:T(8,128)} %bitcast.5, f32[]{:T(128)} %constant.7.clone.1), dimensions={0}, to_apply=%region_0.0 | reduce | flops 3440640 | bytes 15597572 | tf_op jit(solution)/shard_map/reduce_sum | solution.py:10
  324.3 0.1 divide_convert_fusion
  324.4 13.3 %all_gather.15 = bf16[448,1024]{1,0:T(8,128)(2,1)S(1)} all-gather(bf16[448,512]{1,0:T(8,128)(2,1)S(1)} %divide_convert_fusion), channel_id=1, replica_groups=mesh['rows'=2,'feat'=16] {'rows'}, dimensions={1}, use_global_device_ids=true | all-gather | bytes 1376256 | tf_op jit(solution)/shard_map/all_gather | solution.py:29
  337.7 0.0 copy-done
  337.7 0.0 copy-done.2
  337.7 1.6 convolution_select_fusion
  (1 shorter events, 0.0 us)
Async XLA Ops:
  6.5 331.2 %copy-start = (bf16[512,1024]{1,0:T(8,128)(2,1)S(1)}, bf16[512,1024]{1,0:T(8,128)(2,1)}, u32[]{:S(2)}) copy-start(bf16[512,1024]{1,0:T(8,128)(2,1)} %param.8) | copy-start | bytes 3145732
  6.5 180.6 %all-gather.4.cloned.1.call-start = ((), (), s32[]{:S(2)}) async-start(), calls=%async_computation | async-start | bytes 22020096 | tf_op jit(solution)/shard_map/all_gather | solution.py:20
  7.3 196.5 %copy-start.1 = (f32[1024]{0:T(1024)S(1)}, f32[1024]{0:T(1024)}, u32[]{:S(2)}) copy-start(f32[1024]{0:T(1024)} %param.7) | copy-start | bytes 12292
  7.3 309.9 %all-gather.6.cloned.1.call-start = ((), (), s32[]{:S(2)}) async-start(), calls=%async_computation.1 | async-start | bytes 15597568 | tf_op jit(solution)/shard_map/all_gather | solution.py:10
  203.7 134.1 %copy-start.2 = (s32[448]{0:T(512)S(1)}, s32[448]{0:T(512)}, u32[]{:S(2)}) copy-start(s32[448]{0:T(512)} %param.9) | copy-start | bytes 5380
Sparse Core Ops, SparseCore 0:
  8.9 178.2 all-gather.3
  203.8 113.3 all-gather.5

commit v2 on v0

--- a/solution.py
+++ b/solution.py
@@ -12,10 +12,21 @@
     first_column = (lax.axis_index("rows") * feat_groups + lax.axis_index("feat")) * store_count
     columns = first_column + jnp.arange(store_count, dtype=jnp.int32)
     local_dirs = basis.shape[1]
+
+    def part_sources_all(x_in, out_dim):
+        local_now = jnp.concatenate(
+            lax.all_to_all(
+                jnp.stack([x_in] * lax.axis_size("rows")),
+                axis_name="rows",
+                concat_axis=0,
+                split_axis=0,
+            ),
+            axis=out_dim,
+        )
+        return local_now
+
     partial_value = jnp.dot(
-        lax.all_gather(slab_grads, "rows", axis=0, tiled=True),
-        basis,
-        preferred_element_type=jnp.float32,
+        part_sources_all(slab_grads, 0), basis, preferred_element_type=jnp.float32
     )
     summed = lax.psum(partial_value, "feat")
     scales = lax.dynamic_slice_in_dim(

time: 319 us -> 308 us (0.966)
  waiting for transfers between devices: 273 us -> 92.8 us
  blocking collectives: 13.2 us -> 178 us
  other arithmetic: 1.36 us -> 10.4 us
  matrix products: 18.1 us -> 13.2 us
    all_gather x1 -> x0, waiting for transfers between devices: 180 us -> none  [shards(): lax.all_gather(slab_grads, 'rows', axis=0, tiled=True)]
    all_to_all x0 -> x1, blocking collectives: none -> 165 us  [part_sources_all(): lax.all_to_all(jnp.stack([x_in] * lax.axis_size('rows')), axis_name='rows...]
    another operation x0 -> x1, other arithmetic: none -> 9.04 us  [part_sources_all(): jnp.stack([x_in] * lax.axis_size('rows'))]
    dot_general x1, matrix products: 16.5 us -> 11.5 us  [shards(): jnp.dot(part_sources_all(slab_grads, 0), basis, preferred_element_type=jn...]
  transfers between devices with their start and end apart: 2 -> 1, of which waited for: 2 -> 1; matrix products, arithmetic and copies ran while one was open for 0% -> 0% of each run, Pallas kernels for 0% -> 0%
where the time goes in v2:
time: 308 us
  blocking collectives  178 us (58%)
  waiting for transfers between devices  92.8 us (30%)
  between operations  13.4 us (4%)
  matrix products  13.2 us (4%)
  other arithmetic  10.4 us (3%)
    all_to_all x1, blocking collectives, part_sources_all(): lax.all_to_all(jnp.stack([x_in] * lax.axis_size('rows')), axis_name='rows...  165 us
    psum x1, waiting for transfers between devices, shards(): summed = lax.psum(partial_value, 'feat')  92.8 us
    all_gather x1, blocking collectives, shards(): gathered = lax.all_gather(whitened, 'rows', axis=1, tiled=True)  13.2 us
    dot_general x1, matrix products, shards(): jnp.dot(part_sources_all(slab_grads, 0), basis, preferred_element_type=jn...  11.5 us
    another operation x1, other arithmetic, part_sources_all(): jnp.stack([x_in] * lax.axis_size('rows'))  9.04 us
  transfers between devices with their start and end apart: 1, of which 1 were waited for; matrix products, arithmetic and copies ran while one was open for 0% of the time, Pallas kernels for 0%

profile of v2, /device:TPU:0, one launch (start us, length us, event | category | flops | bytes accessed | tf_op | source)
XLA Modules:
  0.0 307.9 jit_solution(6555375980799515568)
XLA Ops:
  6.5 0.0 copy-start
  6.5 0.0 all-reduce.2.cloned.1.call-start
  6.5 9.0 %pad_maximum_fusion = bf16[2,224,16384]{2,1,0:T(8,128)(2,1)S(1)} fusion(bf16[1,224,16384]{2,1,0:T(8,128)(2,1)} %bitcast.7), kind=kLoop, calls=%fused_computation | loop fusion | flops 7340032 | bytes 22020096 | tf_op jit(solution)/shard_map/stack | solution.py:19
  15.6 164.8 %all_to_all.5 = bf16[2,224,16384]{2,1,0:T(8,128)(2,1)S(1)} all-to-all(bf16[2,224,16384]{2,1,0:T(8,128)(2,1)S(1)} %pad_maximum_fusion), channel_id=1, replica_groups=mesh['rows'=2,'feat'=16] {'rows'}, dimensions={0} | all-to-all | bytes 29360128 | tf_op jit(solution)/shard_map/all_to_all | solution.py:18
  180.4 0.0 copy-start.1
  180.4 0.0 copy-start.2
  180.4 11.5 %fusion = f32[448,512]{1,0:T(8,128)} fusion(bf16[448,16384]{1,0:T(8,128)(2,1)S(1)} %bitcast.6, bf16[16384,512]{1,0:T(8,128)(2,1)} %param.6), kind=kOutput, calls=%fused_computation.5 | convolution fusion | flops 7516192768 | bytes 32374784 | tf_op jit(solution)/shard_map/dot_general | solution.py:28
  191.9 0.0 all-reduce.2.cloned.1.call-update
  192.0 0.0 copy-done.1
  192.0 0.1 dynamic-slice_add_fusion
  192.1 92.8 %all-reduce.2.cloned.1.call-done = f32[448,512]{1,0:T(8,128)} async-done(((f32[448,512]{1,0:T(8,128)}), f32[448,512]{1,0:T(8,128)}) %all-reduce.2.cloned.1.call-update) | async-done | bytes 917520 | tf_op jit(solution)/shard_map/psum | solution.py:31
  284.9 1.3 divide_convert_fusion
  286.2 13.2 %all_gather.3 = bf16[448,1024]{1,0:T(8,128)(2,1)S(1)} all-gather(bf16[448,512]{1,0:T(8,128)(2,1)S(1)} %divide_convert_fusion), channel_id=1, replica_groups=mesh['rows'=2,'feat'=16] {'rows'}, dimensions={1}, use_global_device_ids=true | all-gather | bytes 1376256 | tf_op jit(solution)/shard_map/all_gather | solution.py:36
  299.4 0.0 copy-done
  299.4 0.0 copy-done.2
  299.4 1.6 convolution_select_fusion
  (1 shorter events, 0.0 us)
Async XLA Ops:
  6.5 292.9 %copy-start = (bf16[512,1024]{1,0:T(8,128)(2,1)S(1)}, bf16[512,1024]{1,0:T(8,128)(2,1)}, u32[]{:S(2)}) copy-start(bf16[512,1024]{1,0:T(8,128)(2,1)} %param.8) | copy-start | bytes 3145732
  6.5 278.3 %all-reduce.2.cloned.1.call-start = ((), (), s32[]{:S(2)}) async-start(), calls=%async_computation.1 | async-start | bytes 1835008 | tf_op jit(solution)/shard_map/psum | solution.py:31
  180.4 11.6 %copy-start.1 = (f32[1024]{0:T(1024)S(1)}, f32[1024]{0:T(1024)}, u32[]{:S(2)}) copy-start(f32[1024]{0:T(1024)} %param.7) | copy-start | bytes 12292
  180.4 119.0 %copy-start.2 = (s32[448]{0:T(512)S(1)}, s32[448]{0:T(512)}, u32[]{:S(2)}) copy-start(s32[448]{0:T(512)} %param.9) | copy-start | bytes 5380
Sparse Core Ops, SparseCore 0:
  192.1 92.7 all-reduce.1
